TPU v7x, 32 devices: a whole 2x2x4 slice. The times are simulated.
32 devices in a mesh: cp: 4 (over y, x), fsdp: 2 (over core), rep: 4 (over z).
Axes of the slice: x: 2, y: 2, z: 4, core: 2. Of those that a mesh axis runs over, the one named last changes fastest.
Arguments:
- tokens: bfloat16 [16, 2048, 768], P(('fsdp', 'rep'), 'cp'), may hold values from -6 to 6
- segments: int32 [16, 2048], P(('fsdp', 'rep')), may hold values from 0 to 3, never falling along the last dimension, each value on 1 to 1024 neighbouring positions
- g_one: bfloat16 [768], P('fsdp'), may hold values from 0.099609375 to 1.8984375
- b_one: bfloat16 [768], P('fsdp'), may hold values from -3 to 3
- w_qkv: bfloat16 [768, 2304], P('fsdp'), may hold values from -0.21875 to 0.21875
- b_query: bfloat16 [768], P('fsdp'), may hold values from -3 to 3
- b_value: bfloat16 [768], P('fsdp'), may hold values from -3 to 3
- w_out: bfloat16 [768, 768], P('fsdp'), may hold values from -1.75 to 1.75
- b_out: bfloat16 [768], P('fsdp'), may hold values from -3 to 3
- g_two: bfloat16 [768], P('fsdp'), may hold values from 0.099609375 to 1.8984375
- b_two: bfloat16 [768], P('fsdp'), may hold values from -3 to 3
- w_fc: bfloat16 [768, 3072], P('fsdp'), may hold values from -0.21875 to 0.21875
- b_fc: bfloat16 [3072], P('fsdp'), may hold values from -3 to 3
- w_proj: bfloat16 [3072, 768], P('fsdp'), may hold values from -0.109375 to 0.109375
- b_proj: bfloat16 [768], P('fsdp'), may hold values from -3 to 3
- cotangent: bfloat16 [16, 2048, 768], P(('fsdp', 'rep'), 'cp'), may hold values from -6 to 6
Outputs:
- layer_out: bfloat16 [16, 2048, 768], P(('fsdp', 'rep'), 'cp')
- tokens_grad: bfloat16 [16, 2048, 768], P(('fsdp', 'rep'), 'cp')
- dg_one: float32 [768], P('fsdp')
- db_one: float32 [768], P('fsdp')
- dw_qkv: float32 [768, 2304], P('fsdp')
- db_query: float32 [768], P('fsdp')
- db_value: float32 [768], P('fsdp')
- dw_out: float32 [768, 768], P('fsdp')
- db_out: float32 [768], P('fsdp')
- dg_two: float32 [768], P('fsdp')
- db_two: float32 [768], P('fsdp')
- dw_fc: float32 [768, 3072], P('fsdp')
- db_fc: float32 [3072], P('fsdp')
- dw_proj: float32 [3072, 768], P('fsdp')
- db_proj: float32 [768], P('fsdp')
Inputs may be any that keep to these rules, and one draw needn't show every extreme that they name: `segments`: in each sequence the ids never fall, and each document holds 1 to 1024 positions, one document exactly that many.
All inputs are finite; a program needn't handle non-finite values.
Results may differ from a plain program's by a relative error of at most 0.012.
The roundings to bfloat16 on the way count: a program that leaves them out, or rounds other values in their place, can miss the bound.
Values may be sent and summed in bfloat16 or wider, within the bound.
A program may use at most 384 MiB of HBM per device.

v0:
```python
import jax
import jax.numpy as jnp
from jax import lax
from jax.sharding import PartitionSpec as P

HEADS = 12


def layer_norm(value, gain, shift):
    center = value - jnp.mean(value, axis=-1, keepdims=True)
    spread = jnp.mean(center * center, axis=-1, keepdims=True)
    return center * lax.rsqrt(spread + 1e-05) * gain + shift


def gelu_tanh(value):
    return (
        0.5
        * value
        * (1.0 + jnp.tanh(0.7978845608028654 * (value + 0.044715 * value * value * value)))
    )


def inner_rows(left, right):
    return lax.dot_general(
        left, right, (((0,), (0,)), ((), ())), preferred_element_type=jnp.float32
    )


def times_trans(left, right):
    return lax.dot_general(
        left, right, (((1,), (1,)), ((), ())), preferred_element_type=jnp.float32
    )


def body(
    tokens,
    segments,
    g_one,
    b_one,
    w_qkv,
    b_query,
    b_value,
    w_out,
    b_out,
    g_two,
    b_two,
    w_fc,
    b_fc,
    w_proj,
    b_proj,
    cotangent,
):
    seqs, span, width = tokens.shape
    seq_len = segments.shape[1]
    rows = seqs * span
    size = width // HEADS
    scale = size ** (-0.5)
    first_pos = lax.axis_index("cp") * span
    full = (
        lax.all_gather(g_one, "fsdp", axis=0, tiled=True),
        lax.all_gather(b_one, "fsdp", axis=0, tiled=True),
        lax.all_gather(w_qkv, "fsdp", axis=0, tiled=True),
        lax.all_gather(b_query, "fsdp", axis=0, tiled=True),
        lax.all_gather(b_value, "fsdp", axis=0, tiled=True),
        lax.all_gather(w_out, "fsdp", axis=0, tiled=True),
        lax.all_gather(b_out, "fsdp", axis=0, tiled=True),
        lax.all_gather(g_two, "fsdp", axis=0, tiled=True),
        lax.all_gather(b_two, "fsdp", axis=0, tiled=True),
        lax.all_gather(w_fc, "fsdp", axis=0, tiled=True),
        lax.all_gather(b_fc, "fsdp", axis=0, tiled=True),
        lax.all_gather(w_proj, "fsdp", axis=0, tiled=True),
        lax.all_gather(b_proj, "fsdp", axis=0, tiled=True),
    )
    gain_one = full[0].astype(jnp.float32)
    shift_one = full[1].astype(jnp.float32)
    gain_two = full[7].astype(jnp.float32)
    shift_two = full[8].astype(jnp.float32)
    tok_rows = tokens.reshape(rows, width).astype(jnp.float32)
    normed = layer_norm(tok_rows, gain_one, shift_one).astype(jnp.bfloat16)
    qkv_bias = jnp.concatenate([full[3], jnp.zeros_like(full[3]), full[4]]).astype(jnp.float32)
    merged = (jnp.dot(normed, full[2], preferred_element_type=jnp.float32) + qkv_bias).astype(
        jnp.bfloat16
    )
    merged = merged.reshape(seqs, span, 3 * width)
    query = merged[:, :, :width]
    key_loc = merged[:, :, width : 2 * width]
    value_loc = merged[:, :, 2 * width :]
    keys_all, values_all = (
        lax.all_gather(key_loc, "cp", axis=1, tiled=True),
        lax.all_gather(value_loc, "cp", axis=1, tiled=True),
    )
    key_pos = jnp.arange(seq_len)

    def masked_scores(q_rows, k_rows, seq_ids, near_ids):
        length = k_rows.shape[0]
        q_three = q_rows.reshape(span, HEADS, size)
        k_three = k_rows.reshape(length, HEADS, size)
        scores = (
            jnp.einsum("qhd,khd->hqk", q_three, k_three, preferred_element_type=jnp.float32) * scale
        )
        query_ids = lax.dynamic_slice_in_dim(seq_ids, first_pos, span)
        query_pos = first_pos + jnp.arange(span)
        allowed = (query_ids[:, None] == near_ids[None, :]) & (
            key_pos[None, :] <= query_pos[:, None]
        )
        return jnp.where(allowed[None], scores, -1e30)

    def attend(item):
        q_rows, k_rows, v_rows, seq_ids, near_ids = item
        length = k_rows.shape[0]
        scores = masked_scores(q_rows, k_rows, seq_ids, near_ids)
        top = jnp.max(scores, axis=-1, keepdims=True)
        expo = jnp.exp(scores - top)
        total = jnp.sum(expo, axis=-1, keepdims=True)
        probs = (expo / total).astype(jnp.bfloat16)
        mixed = jnp.einsum(
            "hqk,khd->qhd",
            probs,
            v_rows.reshape(length, HEADS, size),
            preferred_element_type=jnp.float32,
        )
        return (
            mixed.reshape(span, width).astype(jnp.bfloat16),
            top[..., 0] + jnp.log(total[..., 0]),
        )

    mixed, log_total = lax.map(attend, (query, keys_all, values_all, segments, segments))
    mixed_rows = mixed.reshape(rows, width)
    branch = jnp.dot(mixed_rows, full[5], preferred_element_type=jnp.float32) + full[6].astype(
        jnp.float32
    )
    resid = tok_rows + branch
    normed_two = layer_norm(resid, gain_two, shift_two).astype(jnp.bfloat16)
    hidden = jnp.dot(normed_two, full[9], preferred_element_type=jnp.float32) + full[10].astype(
        jnp.float32
    )
    active = gelu_tanh(hidden).astype(jnp.bfloat16)
    output = jnp.dot(active, full[11], preferred_element_type=jnp.float32) + full[12].astype(
        jnp.float32
    )
    layer_out = (resid + output).astype(jnp.bfloat16).reshape(seqs, span, width)
    back = (
        lax.all_gather(g_one, "fsdp", axis=0, tiled=True),
        lax.all_gather(b_one, "fsdp", axis=0, tiled=True),
        lax.all_gather(w_qkv, "fsdp", axis=0, tiled=True),
        lax.all_gather(b_query, "fsdp", axis=0, tiled=True),
        lax.all_gather(b_value, "fsdp", axis=0, tiled=True),
        lax.all_gather(w_out, "fsdp", axis=0, tiled=True),
        lax.all_gather(b_out, "fsdp", axis=0, tiled=True),
        lax.all_gather(g_two, "fsdp", axis=0, tiled=True),
        lax.all_gather(b_two, "fsdp", axis=0, tiled=True),
        lax.all_gather(w_fc, "fsdp", axis=0, tiled=True),
        lax.all_gather(b_fc, "fsdp", axis=0, tiled=True),
        lax.all_gather(w_proj, "fsdp", axis=0, tiled=True),
        lax.all_gather(b_proj, "fsdp", axis=0, tiled=True),
    )
    keys_b, values_b = (
        lax.all_gather(key_loc, "cp", axis=1, tiled=True),
        lax.all_gather(value_loc, "cp", axis=1, tiled=True),
    )
    out_grad = cotangent.reshape(rows, width).astype(jnp.float32)
    d_output = out_grad.astype(jnp.bfloat16)
    dw_proj = inner_rows(active, d_output)
    db_proj = jnp.sum(d_output.astype(jnp.float32), axis=0)
    d_active = times_trans(d_output, back[11])
    _, gelu_pull = jax.vjp(gelu_tanh, hidden)
    d_hidden = gelu_pull(d_active)[0].astype(jnp.bfloat16)
    dw_fc = inner_rows(normed_two, d_hidden)
    db_fc = jnp.sum(d_hidden.astype(jnp.float32), axis=0)
    d_normed_two = times_trans(d_hidden, back[9])
    _, norm_pull_two = jax.vjp(
        layer_norm, resid, back[7].astype(jnp.float32), back[8].astype(jnp.float32)
    )
    d_resid_part, dg_two, db_two = norm_pull_two(d_normed_two)
    d_resid = out_grad + d_resid_part
    d_branch = d_resid.astype(jnp.bfloat16)
    dw_out = inner_rows(mixed_rows, d_branch)
    db_out = jnp.sum(d_branch.astype(jnp.float32), axis=0)
    d_mixed = times_trans(d_branch, back[5]).astype(jnp.bfloat16).reshape(seqs, span, width)

    def attend_back(item):
        q_rows, k_rows, v_rows, seq_ids, near_ids, d_rows, lse_rows = item
        length = k_rows.shape[0]
        scores = masked_scores(q_rows, k_rows, seq_ids, near_ids)
        probs = jnp.exp(scores - lse_rows[..., None])
        d_three = d_rows.reshape(span, HEADS, size)
        v_three = v_rows.reshape(length, HEADS, size)
        d_probs = jnp.einsum("qhd,khd->hqk", d_three, v_three, preferred_element_type=jnp.float32)
        delta = jnp.sum(probs * d_probs, axis=-1, keepdims=True)
        d_scores = (probs * (d_probs - delta)).astype(jnp.bfloat16)
        d_query = (
            jnp.einsum(
                "hqk,khd->qhd",
                d_scores,
                k_rows.reshape(length, HEADS, size),
                preferred_element_type=jnp.float32,
            )
            * scale
        )
        d_key = (
            jnp.einsum(
                "hqk,qhd->khd",
                d_scores,
                q_rows.reshape(span, HEADS, size),
                preferred_element_type=jnp.float32,
            )
            * scale
        )
        d_value = jnp.einsum(
            "hqk,qhd->khd", probs.astype(jnp.bfloat16), d_three, preferred_element_type=jnp.float32
        )
        return (
            d_query.reshape(span, width),
            d_key.reshape(length, width),
            d_value.reshape(length, width),
        )

    d_query, d_key_all, d_value_all = lax.map(
        attend_back, (query, keys_b, values_b, segments, segments, d_mixed, log_total)
    )
    d_key, d_value = (
        lax.psum_scatter(d_key_all, "cp", scatter_dimension=1, tiled=True),
        lax.psum_scatter(d_value_all, "cp", scatter_dimension=1, tiled=True),
    )
    d_merged = (
        jnp.concatenate([d_query, d_key, d_value], axis=-1)
        .astype(jnp.bfloat16)
        .reshape(rows, 3 * width)
    )
    d_merged_f = d_merged.astype(jnp.float32)
    db_query = jnp.sum(d_merged_f[:, :width], axis=0)
    db_value = jnp.sum(d_merged_f[:, 2 * width :], axis=0)
    dw_qkv = inner_rows(normed, d_merged)
    d_normed = times_trans(d_merged, back[2])
    _, norm_pull_one = jax.vjp(
        layer_norm, tok_rows, back[0].astype(jnp.float32), back[1].astype(jnp.float32)
    )
    d_tok_part, dg_one, db_one = norm_pull_one(d_normed)
    tokens_grad = (d_resid + d_tok_part).astype(jnp.bfloat16).reshape(seqs, span, width)
    shards = (
        lax.psum_scatter(dg_one, "fsdp", scatter_dimension=0, tiled=True),
        lax.psum_scatter(db_one, "fsdp", scatter_dimension=0, tiled=True),
        lax.psum_scatter(dw_qkv, "fsdp", scatter_dimension=0, tiled=True),
        lax.psum_scatter(db_query, "fsdp", scatter_dimension=0, tiled=True),
        lax.psum_scatter(db_value, "fsdp", scatter_dimension=0, tiled=True),
        lax.psum_scatter(dw_out, "fsdp", scatter_dimension=0, tiled=True),
        lax.psum_scatter(db_out, "fsdp", scatter_dimension=0, tiled=True),
        lax.psum_scatter(dg_two, "fsdp", scatter_dimension=0, tiled=True),
        lax.psum_scatter(db_two, "fsdp", scatter_dimension=0, tiled=True),
        lax.psum_scatter(dw_fc, "fsdp", scatter_dimension=0, tiled=True),
        lax.psum_scatter(db_fc, "fsdp", scatter_dimension=0, tiled=True),
        lax.psum_scatter(dw_proj, "fsdp", scatter_dimension=0, tiled=True),
        lax.psum_scatter(db_proj, "fsdp", scatter_dimension=0, tiled=True),
    )
    totals = lax.psum(
        (
            shards[0],
            shards[1],
            shards[2],
            shards[3],
            shards[4],
            shards[5],
            shards[6],
            shards[7],
            shards[8],
            shards[9],
            shards[10],
            shards[11],
            shards[12],
        ),
        ("cp", "rep"),
    )
    return (
        layer_out,
        tokens_grad,
        totals[0],
        totals[1],
        totals[2],
        totals[3],
        totals[4],
        totals[5],
        totals[6],
        totals[7],
        totals[8],
        totals[9],
        totals[10],
        totals[11],
        totals[12],
    )


def solution(mesh):
    placed = (
        P(("fsdp", "rep"), "cp", None),
        P(("fsdp", "rep"), None),
        P("fsdp"),
        P("fsdp"),
        P("fsdp", None),
        P("fsdp"),
        P("fsdp"),
        P("fsdp", None),
        P("fsdp"),
        P("fsdp"),
        P("fsdp"),
        P("fsdp", None),
        P("fsdp"),
        P("fsdp", None),
        P("fsdp"),
        P(("fsdp", "rep"), "cp", None),
    )
    return jax.shard_map(
        body,
        mesh=mesh,
        in_specs=placed,
        out_specs=(
            P(("fsdp", "rep"), "cp", None),
            P(("fsdp", "rep"), "cp", None),
            P("fsdp"),
            P("fsdp"),
            P("fsdp", None),
            P("fsdp"),
            P("fsdp"),
            P("fsdp", None),
            P("fsdp"),
            P("fsdp"),
            P("fsdp"),
            P("fsdp", None),
            P("fsdp"),
            P("fsdp", None),
            P("fsdp"),
        ),
        check_vma=False,
    )
```

profile of v0, /device:TPU:0, one launch (start us, length us, event | category | flops | bytes accessed | tf_op | source)
XLA Modules:
  0.0 1499.2 jit_solution(1097224443274911993)
XLA Ops:
  50.4 56.1 %all-gather.20.cloned.1.call-done = bf16[2,2048,768]{1,2,0:T(8,128)(2,1)} async-done(((bf16[2,512,768]{1,2,0:T(8,128)(2,1)}), bf16[2,2048,768]{1,2,0:T(8,128)(2,1)}) %all-gather.20.cloned.1.call-update) | async-done | bytes 6291472 | tf_op jit(solution)/shard_map/all_gather | solution.py:89
  106.5 72.5 %all-gather.18.cloned.1.call-done = bf16[2,2048,768]{1,2,0:T(8,128)(2,1)} async-done(((bf16[2,512,768]{1,2,0:T(8,128)(2,1)}), bf16[2,2048,768]{1,2,0:T(8,128)(2,1)}) %all-gather.18.cloned.1.call-update) | async-done | bytes 6291472 | tf_op jit(solution)/shard_map/all_gather | solution.py:90
  178.9 155.2 %while.34 = (s32[]{:T(128)}, bf16[2,512,768]{2,1,0:T(8,128)(2,1)}, f32[2,12,512]{2,1,0:T(8,128)S(1)}, bf16[2,2048,768]{1,2,0:T(8,128)(2,1)}, s32[2,2048]{1,0:T(2...) while((s32[]{:T(128)}, bf16[2,512,768]{2,1,0:T(8,128)(2,1)}, ...), condition=%wide.region_5.6_spmd.clone, body=%wide.region_2.5_spmd.clone.sunk | while | flops 3375753728 | bytes 197388496 | solution.py:127
  188.6 23.9 %fusion.106 = (f32[12,512]{1,0:T(8,128)S(1)}, f32[12,512,2048]{2,1,0:T(8,128)}) fusion(pred[512,2048]{1,0:T(8,128)(4,1)} %fusion.105, bf16[512,12,64]{0,2,1:T(8,128)(2,1)} %bitcast.170, bf16[2048,12,64]{0,2,1:T(8,128)(2,1)S(1)} %bitcast.165), kind=kOutput, calls=%fused_computation.5.clone.1 | convolution fusion | flops 1648355328 | bytes 55336960 | tf_op jit(solution)/shard_map/while/body/eval_jaxpr/qhd,khd->hqk/dot_general | solution.py:99
  212.5 24.5 %fusion.107 = f32[12,512]{1,0:T(8,128)S(1)} fusion(f32[12,512,2048]{2,1,0:T(8,128)} %get-tuple-element.683, f32[12,512]{1,0:T(8,128)S(1)} %get-tuple-element.684, pred[512,2048]{1,0:T(8,128)(4,1)} %fusion.105), kind=kLoop, calls=%fused_computation.6.clone.1 | loop fusion | flops 50325504 | bytes 51429376 | tf_op jit(solution)/shard_map/while/body/eval_jaxpr/reduce_sum | solution.py:114
  237.1 20.2 %fusion.108 = bf16[12,64,512]{2,1,0:T(8,128)(2,1)S(1)} fusion(bf16[2048,12,64]{0,2,1:T(8,128)(2,1)S(1)} %bitcast.174, f32[12,512,2048]{2,1,0:T(8,128)} %get-tuple-element.683, f32[12,512]{1,0:T(8,128)S(1)} %fusion.107, f32[12,512]{1,0:T(8,128)S(1)} %get-tuple-element.684, pred[512,2048]{1,0:T(8,128)(4,1)S(1)} %copy-done), kind=kOutput, calls=%fused_computation.10.clone.1 | convolution fusion | flops 1673920512 | bytes 55361536 | tf_op jit(solution)/shard_map/while/body/eval_jaxpr/hqk,khd->qhd/dot_general | solution.py:116
  268.2 21.5 %fusion.106 = (f32[12,512]{1,0:T(8,128)S(1)}, f32[12,512,2048]{2,1,0:T(8,128)}) fusion(pred[512,2048]{1,0:T(8,128)(4,1)} %fusion.105, bf16[512,12,64]{0,2,1:T(8,128)(2,1)} %bitcast.170, bf16[2048,12,64]{0,2,1:T(8,128)(2,1)S(1)} %bitcast.165), kind=kOutput, calls=%fused_computation.5.clone.1 | convolution fusion | flops 1648355328 | bytes 55336960 | tf_op jit(solution)/shard_map/while/body/eval_jaxpr/qhd,khd->hqk/dot_general | solution.py:99
  289.7 22.9 %fusion.107 = f32[12,512]{1,0:T(8,128)S(1)} fusion(f32[12,512,2048]{2,1,0:T(8,128)} %get-tuple-element.683, f32[12,512]{1,0:T(8,128)S(1)} %get-tuple-element.684, pred[512,2048]{1,0:T(8,128)(4,1)} %fusion.105), kind=kLoop, calls=%fused_computation.6.clone.1 | loop fusion | flops 50325504 | bytes 51429376 | tf_op jit(solution)/shard_map/while/body/eval_jaxpr/reduce_sum | solution.py:114
  312.5 20.2 %fusion.108 = bf16[12,64,512]{2,1,0:T(8,128)(2,1)S(1)} fusion(bf16[2048,12,64]{0,2,1:T(8,128)(2,1)S(1)} %bitcast.174, f32[12,512,2048]{2,1,0:T(8,128)} %get-tuple-element.683, f32[12,512]{1,0:T(8,128)S(1)} %fusion.107, f32[12,512]{1,0:T(8,128)S(1)} %get-tuple-element.684, pred[512,2048]{1,0:T(8,128)(4,1)S(1)} %copy-done), kind=kOutput, calls=%fused_computation.10.clone.1 | convolution fusion | flops 1673920512 | bytes 55361536 | tf_op jit(solution)/shard_map/while/body/eval_jaxpr/hqk,khd->qhd/dot_general | solution.py:116
  379.7 375.4 %while.35 = (s32[]{:T(128)}, bf16[2,512,768]{2,1,0:T(8,128)(2,1)}, f32[2,2048,768]{2,1,0:T(8,128)}, f32[2,2048,768]{2,1,0:T(8,128)}, bf16[2,2048,768]{1,2,0:T(8,...) while((s32[]{:T(128)}, bf16[2,512,768]{2,1,0:T(8,128)(2,1)}, ...), condition=%wide.region_12.13_spmd.clone, body=%wide.region_10.12_spmd.clone.sunk | while | flops 8247306752 | bytes 519514368 | solution.py:218
  392.5 20.5 %fusion.119 = f32[12,512,2048]{2,1,0:T(8,128)} fusion(bf16[512,12,64]{0,2,1:T(8,128)(2,1)} %bitcast.167, bf16[2048,12,64]{0,2,1:T(8,128)(2,1)S(1)} %bitcast.162), kind=kOutput, calls=%fused_computation.114.clone.1 | convolution fusion | flops 1610612736 | bytes 54263808 | tf_op jit(solution)/shard_map/while/body/eval_jaxpr/qhd,khd->hqk/dot_general | solution.py:99
  413.0 23.1 %fusion.121 = f32[12,64,2048]{2,1,0:T(8,128)} fusion(bf16[512,12,64]{0,2,1:T(8,128)(2,1)} %bitcast.172, f32[12,512,2048]{2,1,0:T(8,128)} %fusion.119, f32[12,512]{1,0:T(8,128)S(1)} %dynamic-slice_bitcast_fusion.2, pred[512,2048]{1,0:T(8,128)(4,1)} %fusion.120), kind=kOutput, calls=%fused_computation.24.clone.1 | convolution fusion | flops 1660944384 | bytes 58482688 | tf_op jit(solution)/shard_map/while/body/eval_jaxpr/hqk,qhd->khd/dot_general | solution.py:209
  442.7 37.6 %multiply_reduce_fusion.5 = (f32[12,512]{1,0:T(8,128)S(1)}, f32[12,512,2048]{2,1,0:T(8,128)}) fusion(f32[12,512,2048]{2,1,0:T(8,128)} %fusion.119, f32[12,512]{1,0:T(8,128)S(1)} %dynamic-slice_bitcast_fusion.2, pred[512,2048]{1,0:T(8,128)(4,1)} %fusion.120, bf16[512,12,64]{0,2,1:T(8,128)(2,1)} %bitcast.173, bf16[2048,12,64]{0,2,1:T(8,128)(2,1)} %bitcast.166), kind=kOutput, calls=%fused_computation.21.clone.1 | convolution fusion | flops 1673521152 | bytes 105693184 | tf_op jit(solution)/shard_map/while/body/eval_jaxpr/qhd,khd->hqk/dot_general | solution.py:188
  480.3 41.4 %multiply_convert_fusion.5 = bf16[12,512,2048]{2,1,0:T(8,128)(2,1)} fusion(f32[12,512,2048]{2,1,0:T(8,128)} %get-tuple-element.697, f32[12,512,2048]{2,1,0:T(8,128)} %fusion.119, f32[12,512]{1,0:T(8,128)S(1)} %get-tuple-element.698, f32[12,512]{1,0:T(8,128)S(1)} %dynamic-slice_bitcast_fusion.2, pred[512,2048]{1,0:T(8,128)(4,1)} %fusion.120), kind=kLoop, calls=%fused_computation.20.clone.1 | loop fusion | flops 75497472 | bytes 126926848 | tf_op jit(solution)/shard_map/while/body/eval_jaxpr/convert_element_type | solution.py:190
  578.6 20.5 %fusion.119 = f32[12,512,2048]{2,1,0:T(8,128)} fusion(bf16[512,12,64]{0,2,1:T(8,128)(2,1)} %bitcast.167, bf16[2048,12,64]{0,2,1:T(8,128)(2,1)S(1)} %bitcast.162), kind=kOutput, calls=%fused_computation.114.clone.1 | convolution fusion | flops 1610612736 | bytes 54263808 | tf_op jit(solution)/shard_map/while/body/eval_jaxpr/qhd,khd->hqk/dot_general | solution.py:99
  599.1 23.1 %fusion.121 = f32[12,64,2048]{2,1,0:T(8,128)} fusion(bf16[512,12,64]{0,2,1:T(8,128)(2,1)} %bitcast.172, f32[12,512,2048]{2,1,0:T(8,128)} %fusion.119, f32[12,512]{1,0:T(8,128)S(1)} %dynamic-slice_bitcast_fusion.2, pred[512,2048]{1,0:T(8,128)(4,1)} %fusion.120), kind=kOutput, calls=%fused_computation.24.clone.1 | convolution fusion | flops 1660944384 | bytes 58482688 | tf_op jit(solution)/shard_map/while/body/eval_jaxpr/hqk,qhd->khd/dot_general | solution.py:209
  628.9 37.6 %multiply_reduce_fusion.5 = (f32[12,512]{1,0:T(8,128)S(1)}, f32[12,512,2048]{2,1,0:T(8,128)}) fusion(f32[12,512,2048]{2,1,0:T(8,128)} %fusion.119, f32[12,512]{1,0:T(8,128)S(1)} %dynamic-slice_bitcast_fusion.2, pred[512,2048]{1,0:T(8,128)(4,1)} %fusion.120, bf16[512,12,64]{0,2,1:T(8,128)(2,1)} %bitcast.173, bf16[2048,12,64]{0,2,1:T(8,128)(2,1)} %bitcast.166), kind=kOutput, calls=%fused_computation.21.clone.1 | convolution fusion | flops 1673521152 | bytes 105693184 | tf_op jit(solution)/shard_map/while/body/eval_jaxpr/qhd,khd->hqk/dot_general | solution.py:188
  666.4 41.4 %multiply_convert_fusion.5 = bf16[12,512,2048]{2,1,0:T(8,128)(2,1)} fusion(f32[12,512,2048]{2,1,0:T(8,128)} %get-tuple-element.697, f32[12,512,2048]{2,1,0:T(8,128)} %fusion.119, f32[12,512]{1,0:T(8,128)S(1)} %get-tuple-element.698, f32[12,512]{1,0:T(8,128)S(1)} %dynamic-slice_bitcast_fusion.2, pred[512,2048]{1,0:T(8,128)(4,1)} %fusion.120), kind=kLoop, calls=%fused_computation.20.clone.1 | loop fusion | flops 75497472 | bytes 126926848 | tf_op jit(solution)/shard_map/while/body/eval_jaxpr/convert_element_type | solution.py:190
  787.2 88.8 %reduce-scatter.9.cloned.1.call-done = f32[2,512,768]{2,1,0:T(8,128)} async-done(((f32[2,2048,768]{2,1,0:T(8,128)}), f32[2,512,768]{2,1,0:T(8,128)}) %reduce-scatter.9.cloned.1.call-update) | async-done | bytes 3145744 | tf_op jit(solution)/shard_map/reduce_scatter | solution.py:223
  878.1 121.8 %reduce-scatter.7.cloned.1.call-done = f32[2,512,768]{2,1,0:T(8,128)} async-done(((f32[2,2048,768]{2,1,0:T(8,128)}), f32[2,512,768]{2,1,0:T(8,128)}) %reduce-scatter.7.cloned.1.call-update) | async-done | bytes 3145744 | tf_op jit(solution)/shard_map/reduce_scatter | solution.py:222
  1012.7 21.2 %reduce-scatter.15.cloned.1.call-done = f32[384,3072]{1,0:T(8,128)} async-done(((f32[768,3072]{1,0:T(8,128)}), f32[384,3072]{1,0:T(8,128)}) %reduce-scatter.15.cloned.1.call-update) | async-done | bytes 4718608 | tf_op jit(solution)/shard_map/reduce_scatter | solution.py:250
  1033.9 21.5 %reduce-scatter.17.cloned.1.call-done = f32[1536,768]{1,0:T(8,128)} async-done(((f32[3072,768]{1,0:T(8,128)}), f32[1536,768]{1,0:T(8,128)}) %reduce-scatter.17.cloned.1.call-update) | async-done | bytes 4718608 | tf_op jit(solution)/shard_map/reduce_scatter | solution.py:252
  1108.0 82.4 %all-reduce.9 = (f32[384]{0:T(512)}, f32[384]{0:T(512)}, f32[384]{0:T(512)}, f32[384]{0:T(512)}, f32[384]{0:T(512)}, /*index=5*/f32[384]{0:T(512)}, f32[384]{0:T(512)}, f32[1536]{0:T(1024)}, f32[384]{0:T(512)}) all-reduce(f32[384]{0:T(512)S(1)} %dynamic-slice.11, ...), channel_id=1, replica_groups=mesh['cp'=4,'fsdp'=2,'rep'=4] {'cp','rep'}, use_global_device_ids=true, to_apply=%region_19.20 | all-reduce | flops 4608 | bytes 36864 | tf_op jit(solution)/shard_map/psum | solution.py:255
  1195.0 286.7 %all-reduce.14.cloned.1.call-done = (f32[384,2304]{1,0:T(8,128)}, f32[384,768]{1,0:T(8,128)}, f32[384,3072]{1,0:T(8,128)}, f32[1536,768]{1,0:T(8,128)}) async-done(((f32[384,2304]{1,0:T(8,128)}, f32[384,768]{1,0:T(8,128)}, f32[384,3072]{1,0:T(8,128)}, f32[1536,768]{1,0:T(8,128)}), (f32[384,2304]{1,0:T(8,128)}, f32[384,768]{1,0:T(8,128)}, f32[384,3072]{1,0:T(8,128)}, ...) | async-done | bytes 14155792 | tf_op jit(solution)/shard_map/psum | solution.py:255
  (319 shorter events, 350.1 us)
Async XLA Ops:
  7.2 17.8 %all-gather.16.cloned.1.call-start = ((), (), s32[]{:S(2)}) async-start(), calls=%async_computation.6 | async-start | bytes 5308416 | tf_op jit(solution)/shard_map/all_gather | solution.py:62
  7.9 98.5 %all-gather.20.cloned.1.call-start = ((), (), s32[]{:S(2)}) async-start(), calls=%async_computation.8 | async-start | bytes 7864320 | tf_op jit(solution)/shard_map/all_gather | solution.py:89
  35.1 143.8 %all-gather.18.cloned.1.call-start = ((), (), s32[]{:S(2)}) async-start(), calls=%async_computation.7 | async-start | bytes 7864320 | tf_op jit(solution)/shard_map/all_gather | solution.py:90
  36.8 297.3 %all-gather.22.cloned.1.call-start = ((), (), s32[]{:S(2)}) async-start(), calls=%async_computation.9 | async-start | bytes 1769472 | tf_op jit(solution)/shard_map/all_gather | solution.py:65
  37.4 141.6 %copy-start.23 = (s32[2,2048]{1,0:T(2,128)S(1)}, s32[2,2048]{1,0:T(2,128)}, u32[]{:S(2)}) copy-start(s32[2,2048]{1,0:T(2,128)} %param.21) | copy-start | bytes 49156
  37.4 301.1 %all-gather.24.cloned.1.call-start = ((), (), s32[]{:S(2)}) async-start(), calls=%async_computation.10 | async-start | bytes 7077888 | tf_op jit(solution)/shard_map/all_gather | solution.py:69
  38.0 311.6 %all-gather.26.cloned.1.call-start = ((), (), s32[]{:S(2)}) async-start(), calls=%async_computation.11 | async-start | bytes 7077888 | tf_op jit(solution)/shard_map/all_gather | solution.py:71
  38.5 837.5 %reduce-scatter.9.cloned.1.call-start = ((), (), s32[]{:S(2)}) async-start(), calls=%async_computation.13 | async-start | bytes 15728640 | tf_op jit(solution)/shard_map/reduce_scatter | solution.py:223
  178.9 155.2 %copy-start.46 = (f32[768]{0:T(1024)S(1)}, f32[768]{0:T(1024)}, u32[]{:S(2)}) copy-start(f32[768]{0:T(1024)} %reshape.447) | copy-start | bytes 9220
  212.5 24.5 %copy-start = (pred[512,2048]{1,0:T(8,128)(4,1)S(1)}, pred[512,2048]{1,0:T(8,128)(4,1)}, u32[]{:S(2)}) copy-start(pred[512,2048]{1,0:T(8,128)(4,1)} %fusion.105) | copy-start | bytes 3145732 | tf_op jit(solution)/shard_map/while
  212.5 24.5 %copy-start.3 = (bf16[1,2048,768]{1,2,0:T(8,128)(2,1)S(1)}, bf16[1,2048,768]{1,2,0:T(8,128)(2,1)}, u32[]{:S(2)}) copy-start(bf16[1,2048,768]{1,2,0:T(8,128)(2,1)} %get-tuple-element.681) | copy-start | bytes 9437188 | tf_op jit(solution)/shard_map/while
  289.6 22.9 %copy-start = (pred[512,2048]{1,0:T(8,128)(4,1)S(1)}, pred[512,2048]{1,0:T(8,128)(4,1)}, u32[]{:S(2)}) copy-start(pred[512,2048]{1,0:T(8,128)(4,1)} %fusion.105) | copy-start | bytes 3145732 | tf_op jit(solution)/shard_map/while
  289.6 22.9 %copy-start.3 = (bf16[1,2048,768]{1,2,0:T(8,128)(2,1)S(1)}, bf16[1,2048,768]{1,2,0:T(8,128)(2,1)}, u32[]{:S(2)}) copy-start(bf16[1,2048,768]{1,2,0:T(8,128)(2,1)} %get-tuple-element.681) | copy-start | bytes 9437188 | tf_op jit(solution)/shard_map/while
  337.9 36.6 %copy-start.6 = (f32[1024,768]{1,0:T(8,128)}, f32[1024,768]{1,0:T(8,128)S(1)}, u32[]{:S(2)}) copy-start(f32[1024,768]{1,0:T(8,128)S(1)} %get-tuple-element.552) | copy-start | bytes 9437188
  338.0 36.6 %copy-start.24 = (f32[1024]{0:T(1024)}, f32[1024]{0:T(1024)S(1)}, u32[]{:S(2)}) copy-start(f32[1024]{0:T(1024)S(1)} %broadcast_multiply_fusion) | copy-start | bytes 12292
  338.5 36.1 %copy-start.26 = (f32[1024]{0:T(1024)}, f32[1024]{0:T(1024)S(1)}, u32[]{:S(2)}) copy-start(f32[1024]{0:T(1024)S(1)} %fusion.36) | copy-start | bytes 12292
  755.1 244.8 %reduce-scatter.7.cloned.1.call-start = ((), (), s32[]{:S(2)}) async-start(), calls=%async_computation.12 | async-start | bytes 15728640 | tf_op jit(solution)/shard_map/reduce_scatter | solution.py:222
  755.9 256.8 %reduce-scatter.13.cloned.1.call-start = ((), (), s32[]{:S(2)}) async-start(), calls=%async_computation.15 | async-start | bytes 3538944 | tf_op jit(solution)/shard_map/reduce_scatter | solution.py:246
  760.9 273.0 %reduce-scatter.15.cloned.1.call-start = ((), (), s32[]{:S(2)}) async-start(), calls=%async_computation.16 | async-start | bytes 14155776 | tf_op jit(solution)/shard_map/reduce_scatter | solution.py:250
  772.6 282.7 %reduce-scatter.17.cloned.1.call-start = ((), (), s32[]{:S(2)}) async-start(), calls=%async_computation.17 | async-start | bytes 14155776 | tf_op jit(solution)/shard_map/reduce_scatter | solution.py:252
  787.0 287.5 %reduce-scatter.11.cloned.1.call-start = ((), (), s32[]{:S(2)}) async-start(), calls=%async_computation.14 | async-start | bytes 10616832 | tf_op jit(solution)/shard_map/reduce_scatter | solution.py:243
  878.1 133.4 %copy-start.15 = (bf16[2,512,768]{2,1,0:T(8,128)(2,1)}, bf16[2,512,768]{2,1,0:T(8,128)(2,1)S(1)}, u32[]{:S(2)}) copy-start(bf16[2,512,768]{2,1,0:T(8,128)(2,1)S(1)} %convert.15) | copy-start | bytes 4718596
  1011.5 470.1 %all-reduce.14.cloned.1.call-start = ((), (), s32[]{:S(2)}) async-start(), calls=%async_computation.18 | async-start | bytes 28311552 | tf_op jit(solution)/shard_map/psum | solution.py:255
  1101.7 88.7 %copy-start.39 = (f32[1024]{0:T(1024)S(1)}, f32[1024]{0:T(1024)}, u32[]{:S(2)}) copy-start(f32[1024]{0:T(1024)} %copy-done.38) | copy-start | bytes 12292
  (57 other events, 347.4 us)
Sparse Core Ops, SparseCore 0:
  9.6 15.3 all-gather.15
  35.2 71.1 all-gather.19
  108.9 70.0 all-gather.17
  180.3 9.2 all-gather.21
  191.0 15.5 all-gather.23
  208.0 15.6 all-gather.25
  755.2 120.7 reduce-scatter.8
  879.2 120.7 reduce-scatter.6
  1002.8 9.8 reduce-scatter.12
  1014.9 18.9 reduce-scatter.14
  1036.3 19.0 reduce-scatter.16
  1057.7 16.8 reduce-scatter.10
  1081.0 400.6 all-reduce.13
where the time goes:
time: 1500 us
  waiting for transfers between devices  695 us (46%)
  matrix products  410 us (27%)
  other arithmetic  160 us (11%)
  local copies, waits for them, and re-layouts  111 us (7%)
  blocking collectives  103 us (7%)
  between operations  16.3 us (1%)
    psum x1, waiting for transfers between devices, body(): lax.psum((shards[0], shards[1], shards[2], shards[3], shards[4], shards[5...  287 us
    reduce_scatter x1, waiting for transfers between devices, body(): lax.psum_scatter(d_key_all, 'cp', scatter_dimension=1, tiled=True)  122 us
    reduce_scatter x1, waiting for transfers between devices, body(): lax.psum_scatter(d_value_all, 'cp', scatter_dimension=1, tiled=True)  88.8 us
    dot_general x4, matrix products, masked_scores(): jnp.einsum('qhd,khd->hqk', q_three, k_three, preferred_element_type=jnp.f...  86.3 us
    convert_element_type x2, other arithmetic, attend_back(): d_scores = (probs * (d_probs - delta)).astype(jnp.bfloat16)  82.8 us
    psum x1, blocking collectives, body(): lax.psum((shards[0], shards[1], shards[2], shards[3], shards[4], shards[5...  82.4 us
    dot_general x2, matrix products, attend_back(): jnp.einsum('qhd,khd->hqk', d_three, v_three, preferred_element_type=jnp.f...  75.1 us
    all_gather x1, waiting for transfers between devices, body(): lax.all_gather(value_loc, 'cp', axis=1, tiled=True)  72.5 us
  transfers between devices with their start and end apart: 13, of which 10 were waited for; matrix products, arithmetic and copies ran while one was open for 17% of the time, Pallas kernels for 0%

commit v1 on v0

v1 whole, which is shorter than its diff:
```python
import jax
import jax.numpy as jnp
from jax import lax
from jax.experimental import pallas as pl
from jax.experimental.pallas import tpu as pltpu
from jax.sharding import PartitionSpec as P

HEADS = 12


def layer_norm(value, gain, shift):
    center = value - jnp.mean(value, axis=-1, keepdims=True)
    spread = jnp.mean(center * center, axis=-1, keepdims=True)
    return center * lax.rsqrt(spread + 1e-05) * gain + shift


def gelu_tanh(value):
    return (
        0.5
        * value
        * (1.0 + jnp.tanh(0.7978845608028654 * (value + 0.044715 * value * value * value)))
    )


def inner_rows(left, right):
    return lax.dot_general(
        left, right, (((0,), (0,)), ((), ())), preferred_element_type=jnp.float32
    )


def times_trans(left, right):
    return lax.dot_general(
        left, right, (((1,), (1,)), ((), ())), preferred_element_type=jnp.float32
    )


BLOCK = 256
NEG = -1e30


def dot_nt(left, right):
    return lax.dot_general(
        left, right, (((1,), (1,)), ((), ())), preferred_element_type=jnp.float32
    )


def dot_tn(left, right):
    return lax.dot_general(
        left, right, (((0,), (0,)), ((), ())), preferred_element_type=jnp.float32
    )


def block_at(ref, index, per, low, high):
    row = pl.multiple_of((index % per) * BLOCK, BLOCK)
    return ref[index // per, pl.ds(row, BLOCK), low:high]


def mask_of(i, j, starts, diagonal):
    near = j * BLOCK + lax.broadcasted_iota(jnp.int32, (BLOCK, BLOCK), 0)
    allowed = near >= starts
    if diagonal:
        mine = i * BLOCK + lax.broadcasted_iota(jnp.int32, (BLOCK, BLOCK), 1)
        allowed = allowed & (near <= mine)
    return allowed


def attend_kernel(low_ref, start_ref, qkv_ref, out_ref, wide_ref, lse_ref, *, heads, size, per):
    seq = pl.program_id(0)
    group = heads * size
    blocks = start_ref.shape[1] // BLOCK
    scale = size ** (-0.5)

    def one_block(i, _):
        cols = pl.ds(pl.multiple_of(i * BLOCK, BLOCK), BLOCK)
        starts = start_ref[:, cols]
        query = [
            block_at(qkv_ref, i, per, h * size, (h + 1) * size) * jnp.bfloat16(scale)
            for h in range(heads)
        ]

        def step(j, carry, diagonal):
            allowed = mask_of(i, j, starts, diagonal)
            state = []
            for h in range(heads):
                keys = block_at(qkv_ref, j, per, group + h * size, group + (h + 1) * size)
                values = block_at(qkv_ref, j, per, 2 * group + h * size, 2 * group + (h + 1) * size)
                scores = jnp.where(allowed, dot_nt(keys, query[h]), NEG)
                best = jnp.max(scores, axis=0, keepdims=True)
                if carry is None:
                    expo = jnp.exp(scores - best)
                    total = jnp.sum(expo, axis=0, keepdims=True)
                    mixed = dot_tn(values, expo.astype(jnp.bfloat16))
                else:
                    top, total, mixed = carry[h]
                    best = jnp.maximum(best, top)
                    shrink = jnp.exp(top - best)
                    expo = jnp.exp(scores - best)
                    total = total * shrink + jnp.sum(expo, axis=0, keepdims=True)
                    mixed = mixed * shrink + dot_tn(values, expo.astype(jnp.bfloat16))
                state.append((best, total, mixed))
            return tuple(state)

        state = step(i, None, True)
        state = lax.fori_loop(low_ref[seq, i], i, lambda j, c: step(j, c, False), state)
        wide = jnp.concatenate([mixed / total for _, total, mixed in state], axis=0)
        wide_ref[:, cols] = wide
        for h in range(heads):
            lse_ref[h : h + 1, cols] = state[h][0] + jnp.log(state[h][1])
        row = pl.multiple_of((i % per) * BLOCK, BLOCK)
        out_ref[i // per, pl.ds(row, BLOCK), :] = wide.T.astype(jnp.bfloat16)
        return 0

    lax.fori_loop(0, blocks, one_block, 0)


def back_kernel(
    low_ref,
    start_ref,
    qkv_ref,
    grad_ref,
    wide_ref,
    lse_ref,
    out_ref,
    dq_ref,
    dk_ref,
    dv_ref,
    *,
    heads,
    size,
    per,
):
    seq = pl.program_id(0)
    group = heads * size
    blocks = start_ref.shape[1] // BLOCK
    scale = size ** (-0.5)

    def one_block(i, _):
        cols = pl.ds(pl.multiple_of(i * BLOCK, BLOCK), BLOCK)
        starts = start_ref[:, cols]
        row = pl.multiple_of((i % per) * BLOCK, BLOCK)
        grad_t = grad_ref[i // per, pl.ds(row, BLOCK), :].astype(jnp.float32).T
        prod = grad_t * wide_ref[:, cols]
        query, grads, lse, delta = [], [], [], []
        for h in range(heads):
            query.append(
                block_at(qkv_ref, i, per, h * size, (h + 1) * size) * jnp.bfloat16(scale)
            )
            grads.append(block_at(grad_ref, i, per, h * size, (h + 1) * size))
            lse.append(lse_ref[h : h + 1, cols])
            delta.append(jnp.sum(prod[h * size : (h + 1) * size], axis=0, keepdims=True))

        def step(j, carry, diagonal):
            allowed = mask_of(i, j, starts, diagonal)
            rows = pl.ds(pl.multiple_of(j * BLOCK, BLOCK), BLOCK)
            state = []
            for h in range(heads):
                keys = block_at(qkv_ref, j, per, group + h * size, group + (h + 1) * size)
                values = block_at(qkv_ref, j, per, 2 * group + h * size, 2 * group + (h + 1) * size)
                scores = jnp.where(allowed, dot_nt(keys, query[h]), NEG)
                probs = jnp.exp(scores - lse[h])
                d_probs = dot_nt(values, grads[h])
                d_scores = (probs * (d_probs - delta[h])).astype(jnp.bfloat16)
                d_value = jnp.dot(
                    probs.astype(jnp.bfloat16), grads[h], preferred_element_type=jnp.float32
                )
                d_key = jnp.dot(d_scores, query[h], preferred_element_type=jnp.float32)
                d_query = dot_tn(keys, d_scores)
                if diagonal:
                    dk_ref[h, rows, :] = d_key
                    dv_ref[h, rows, :] = d_value
                    state.append(d_query)
                else:
                    dk_ref[h, rows, :] += d_key
                    dv_ref[h, rows, :] += d_value
                    state.append(carry[h] + d_query)
            return tuple(state)

        state = step(i, None, True)
        state = lax.fori_loop(low_ref[seq, i], i, lambda j, c: step(j, c, False), state)
        dq_ref[:, cols] = jnp.concatenate(state, axis=0) * scale
        return 0

    lax.fori_loop(0, blocks, one_block, 0)

    def finish(i, _):
        cols = pl.ds(pl.multiple_of(i * BLOCK, BLOCK), BLOCK)
        row = pl.multiple_of((i % per) * BLOCK, BLOCK)
        parts = [dq_ref[:, cols].T.astype(jnp.bfloat16)]
        parts += [dk_ref[h, cols, :].astype(jnp.bfloat16) for h in range(heads)]
        parts += [dv_ref[h, cols, :].astype(jnp.bfloat16) for h in range(heads)]
        out_ref[i // per, pl.ds(row, BLOCK), :] = jnp.concatenate(parts, axis=1)
        return 0

    lax.fori_loop(0, blocks, finish, 0)


def attend(low, starts, qkv, heads, size):
    ways, seqs, span, three = qkv.shape
    length = ways * span
    group = heads * size
    part = lambda cols: pl.BlockSpec((ways, None, span, cols), lambda s, low: (0, s, 0, 0))
    rows = lambda count: pl.BlockSpec((None, count, length), lambda s, low: (s, 0, 0))
    return pl.pallas_call(
        lambda *refs: attend_kernel(*refs, heads=heads, size=size, per=span // BLOCK),
        name="attend",
        out_shape=(
            jax.ShapeDtypeStruct((ways, seqs, span, group), jnp.bfloat16),
            jax.ShapeDtypeStruct((seqs, group, length), jnp.float32),
            jax.ShapeDtypeStruct((seqs, heads, length), jnp.float32),
        ),
        grid_spec=pltpu.PrefetchScalarGridSpec(
            num_scalar_prefetch=1,
            grid=(seqs,),
            in_specs=[rows(1), part(three)],
            out_specs=[part(group), rows(group), rows(heads)],
        ),
        compiler_params=pltpu.CompilerParams(
            dimension_semantics=("arbitrary",), vmem_limit_bytes=40 << 20
        ),
        cost_estimate=pl.CostEstimate(
            flops=20_000_000_000, bytes_accessed=12_000_000, transcendentals=10_000_000
        ),
    )(low, starts, qkv)


def attend_back(low, starts, qkv, grad, wide, lse, heads, size):
    ways, seqs, span, three = qkv.shape
    length = ways * span
    group = heads * size
    part = lambda cols: pl.BlockSpec((ways, None, span, cols), lambda s, low: (0, s, 0, 0))
    rows = lambda count: pl.BlockSpec((None, count, length), lambda s, low: (s, 0, 0))
    return pl.pallas_call(
        lambda *refs: back_kernel(*refs, heads=heads, size=size, per=span // BLOCK),
        name="attend_back",
        out_shape=jax.ShapeDtypeStruct((ways, seqs, span, three), jnp.bfloat16),
        grid_spec=pltpu.PrefetchScalarGridSpec(
            num_scalar_prefetch=1,
            grid=(seqs,),
            in_specs=[rows(1), part(three), part(group), rows(group), rows(heads)],
            out_specs=part(three),
            scratch_shapes=[
                pltpu.VMEM((group, length), jnp.float32),
                pltpu.VMEM((heads, length, size), jnp.float32),
                pltpu.VMEM((heads, length, size), jnp.float32),
            ],
        ),
        compiler_params=pltpu.CompilerParams(
            dimension_semantics=("arbitrary",), vmem_limit_bytes=48 << 20
        ),
        cost_estimate=pl.CostEstimate(
            flops=50_000_000_000, bytes_accessed=18_000_000, transcendentals=10_000_000
        ),
    )(low, starts, qkv, grad, wide, lse)


def swap(value):
    return lax.all_to_all(value, "cp", 0, 0, tiled=True)


def body(
    tokens,
    segments,
    g_one,
    b_one,
    w_qkv,
    b_query,
    b_value,
    w_out,
    b_out,
    g_two,
    b_two,
    w_fc,
    b_fc,
    w_proj,
    b_proj,
    cotangent,
):
    seqs, span, width = tokens.shape
    rows = seqs * span
    size = width // HEADS
    ways = lax.axis_size("cp")
    heads = HEADS // ways
    group = heads * size

    vectors = (g_one, b_one, b_query, b_value, b_out, g_two, b_two, b_proj, b_fc)
    packed = lax.all_gather(jnp.concatenate(vectors), "fsdp", axis=0)
    vecs, at = [], 0
    for vector in vectors:
        vecs.append(packed[:, at : at + vector.shape[0]].reshape(-1).astype(jnp.float32))
        at += vector.shape[0]
    gain_one, shift_one, bias_q, bias_v, bias_out, gain_two, shift_two, bias_proj, bias_fc = vecs
    full_qkv = lax.all_gather(w_qkv, "fsdp", axis=0, tiled=True)
    full_out = lax.all_gather(w_out, "fsdp", axis=0, tiled=True)
    full_fc = lax.all_gather(w_fc, "fsdp", axis=0, tiled=True)
    full_proj = lax.all_gather(w_proj, "fsdp", axis=0, tiled=True)

    starts = sum(
        jnp.where(segments > v, jnp.sum(segments == v, axis=1, keepdims=True), 0)
        for v in range(3)
    ).astype(jnp.int32)
    low = starts[:, ::BLOCK] // BLOCK
    starts = starts[:, None, :]

    tok_rows = tokens.reshape(rows, width).astype(jnp.float32)
    normed = layer_norm(tok_rows, gain_one, shift_one).astype(jnp.bfloat16)
    qkv_bias = jnp.concatenate([bias_q, jnp.zeros_like(bias_q), bias_v])
    merged = (jnp.dot(normed, full_qkv, preferred_element_type=jnp.float32) + qkv_bias).astype(
        jnp.bfloat16
    )
    merged = merged.reshape(rows, 3, ways, group).transpose(2, 0, 1, 3)
    qkv = swap(merged.reshape(ways, seqs, span, 3 * group))
    mixed, wide, lse = attend(low, starts, qkv, heads, size)
    mixed_rows = swap(mixed).reshape(ways, rows, group).transpose(1, 0, 2).reshape(rows, width)

    branch = jnp.dot(mixed_rows, full_out, preferred_element_type=jnp.float32) + bias_out
    resid = tok_rows + branch
    normed_two = layer_norm(resid, gain_two, shift_two).astype(jnp.bfloat16)
    hidden = jnp.dot(normed_two, full_fc, preferred_element_type=jnp.float32) + bias_fc
    active = gelu_tanh(hidden).astype(jnp.bfloat16)
    output = jnp.dot(active, full_proj, preferred_element_type=jnp.float32) + bias_proj
    layer_out = (resid + output).astype(jnp.bfloat16).reshape(seqs, span, width)

    d_output = cotangent.reshape(rows, width)
    out_grad = d_output.astype(jnp.float32)
    db_proj = jnp.sum(out_grad, axis=0)
    d_active = times_trans(d_output, full_proj)
    _, gelu_pull = jax.vjp(gelu_tanh, hidden)
    d_hidden = gelu_pull(d_active)[0].astype(jnp.bfloat16)
    db_fc = jnp.sum(d_hidden.astype(jnp.float32), axis=0)
    d_normed_two = times_trans(d_hidden, full_fc)
    _, norm_pull_two = jax.vjp(layer_norm, resid, gain_two, shift_two)
    d_resid_part, dg_two, db_two = norm_pull_two(d_normed_two)
    d_resid = out_grad + d_resid_part
    d_branch = d_resid.astype(jnp.bfloat16)
    db_out = jnp.sum(d_branch.astype(jnp.float32), axis=0)
    d_mixed = times_trans(d_branch, full_out).astype(jnp.bfloat16)
    d_mixed = (
        d_mixed.reshape(rows, ways, group).transpose(1, 0, 2).reshape(ways, seqs, span, group)
    )

    def scattered(grad):
        return lax.psum_scatter(grad, "fsdp", scatter_dimension=0, tiled=True)

    dw_proj = scattered(inner_rows(active, d_output).astype(jnp.bfloat16))
    dw_fc = scattered(inner_rows(normed_two, d_hidden).astype(jnp.bfloat16))
    d_mixed = swap(d_mixed)

    d_qkv = swap(attend_back(low, starts, qkv, d_mixed, wide, lse, heads, size))
    d_merged = (
        d_qkv.reshape(ways, rows, 3, group).transpose(1, 2, 0, 3).reshape(rows, 3 * width)
    )
    dw_qkv = scattered(inner_rows(normed, d_merged).astype(jnp.bfloat16))
    d_merged_sum = jnp.sum(d_merged.astype(jnp.float32), axis=0)
    db_query = d_merged_sum[:width]
    db_value = d_merged_sum[2 * width :]
    d_normed = times_trans(d_merged, full_qkv)
    _, norm_pull_one = jax.vjp(layer_norm, tok_rows, gain_one, shift_one)
    d_tok_part, dg_one, db_one = norm_pull_one(d_normed)
    tokens_grad = (d_resid + d_tok_part).astype(jnp.bfloat16).reshape(seqs, span, width)

    small = (dg_one, db_one, db_query, db_value, db_out, dg_two, db_two, db_proj, db_fc)
    shards = lax.axis_size("fsdp")
    flat = jnp.concatenate([grad.reshape(shards, -1) for grad in small], axis=1)
    count = flat.shape[1]
    extra = 16 * pl.cdiv(count, 16 * width)
    flat = jnp.pad(flat, ((0, 0), (0, extra * width - count))).reshape(shards, extra, width)
    dw_out = inner_rows(mixed_rows, d_branch).reshape(shards, -1, width)
    both = jnp.concatenate([dw_out, flat], axis=1).reshape(-1, width)
    both = scattered(both.astype(jnp.bfloat16))
    sums = lax.psum((dw_qkv, both, dw_fc, dw_proj), ("cp", "rep"))
    dw_qkv, both, dw_fc, dw_proj = [part.astype(jnp.float32) for part in sums]
    dw_out, flat = both[: width // shards], both[width // shards :].reshape(-1)
    own, at = [], 0
    for vector in vectors:
        own.append(flat[at : at + vector.shape[0]])
        at += vector.shape[0]
    dg_one, db_one, db_query, db_value, db_out, dg_two, db_two, db_proj, db_fc = own
    return (
        layer_out,
        tokens_grad,
        dg_one,
        db_one,
        dw_qkv,
        db_query,
        db_value,
        dw_out,
        db_out,
        dg_two,
        db_two,
        dw_fc,
        db_fc,
        dw_proj,
        db_proj,
    )


def solution(mesh):
    placed = (
        P(("fsdp", "rep"), "cp", None),
        P(("fsdp", "rep"), None),
        P("fsdp"),
        P("fsdp"),
        P("fsdp", None),
        P("fsdp"),
        P("fsdp"),
        P("fsdp", None),
        P("fsdp"),
        P("fsdp"),
        P("fsdp"),
        P("fsdp", None),
        P("fsdp"),
        P("fsdp", None),
        P("fsdp"),
        P(("fsdp", "rep"), "cp", None),
    )
    return jax.shard_map(
        body,
        mesh=mesh,
        in_specs=placed,
        out_specs=(
            P(("fsdp", "rep"), "cp", None),
            P(("fsdp", "rep"), "cp", None),
            P("fsdp"),
            P("fsdp"),
            P("fsdp", None),
            P("fsdp"),
            P("fsdp"),
            P("fsdp", None),
            P("fsdp"),
            P("fsdp"),
            P("fsdp"),
            P("fsdp", None),
            P("fsdp"),
            P("fsdp", None),
            P("fsdp"),
        ),
        check_vma=False,
    )
```

time: 1500 us -> 752 us (0.50)
  matrix products: 410 us -> 99.4 us
  waiting for transfers between devices: 695 us -> 388 us
  other arithmetic: 160 us -> 25.5 us
  Pallas kernels: 0 us -> 86.1 us
  blocking collectives: 103 us -> 24.4 us
  local copies, waits for them, and re-layouts: 111 us -> 92.1 us
  starting transfers between devices: 0.69 us -> 15.9 us
    dot_general x18 -> x4, matrix products: 340 us -> 35.7 us  [the longest x1 13.7 us: body(): jnp.dot(active, full_proj, preferred_element_type=jnp.float32) + bias_proj]
    reduce_scatter x6 -> x4, waiting for transfers between devices: 274 us -> 39.9 us  [scattered(): return lax.psum_scatter(grad, 'fsdp', scatter_dimension=0, tiled=True)]
    all_gather x6 -> x4, waiting for transfers between devices: 132 us -> 8.39 us  [the longest x1 8.39 us: body(): full_qkv = lax.all_gather(w_qkv, 'fsdp', axis=0, tiled=True)]
    all_to_all x0 -> x3, waiting for transfers between devices: none -> 115 us  [swap(): return lax.all_to_all(value, 'cp', 0, 0, tiled=True)]
    pallas_call x0 -> x2, Pallas kernels: none -> 86.1 us  [the longest x1 43.5 us: attend(): pl.pallas_call(lambda *refs: attend_kernel(*refs, heads=heads, size=size,...]
    psum x1 -> x0, blocking collectives: 82.4 us -> none  [body(): lax.psum((shards[0], shards[1], shards[2], shards[3], shards[4], shards[5...]
    convert_element_type x11 -> x5, other arithmetic: 86.4 us -> 9.74 us  [the longest x3 9.14 us: body(): dw_qkv, both, dw_fc, dw_proj = [part.astype(jnp.float32) for part in sums]]
    psum x1, waiting for transfers between devices: 287 us -> 222 us  [body(): sums = lax.psum((dw_qkv, both, dw_fc, dw_proj), ('cp', 'rep'))]
  transfers between devices with their start and end apart: 13 -> 12, of which waited for: 10 -> 8; matrix products, arithmetic and copies ran while one was open for 17% -> 16% of each run, Pallas kernels for 0% -> 6%
where the time goes in v1:
time: 752 us; the launch traced here: 746 us
  waiting for transfers between devices  388 us (52%)
  matrix products  99.4 us (13%)
  local copies, waits for them, and re-layouts  92.1 us (12%)
  Pallas kernels  86.1 us (11%)
  other arithmetic  25.5 us (3%)
  blocking collectives  24.4 us (3%)
  starting transfers between devices  15.9 us (2%)
  between operations  14.6 us (2%)
    psum x1, waiting for transfers between devices, body(): sums = lax.psum((dw_qkv, both, dw_fc, dw_proj), ('cp', 'rep'))  222 us
    all_to_all x3, waiting for transfers between devices, swap(): return lax.all_to_all(value, 'cp', 0, 0, tiled=True)  115 us
    pallas_call x1, Pallas kernels, attend(): pl.pallas_call(lambda *refs: attend_kernel(*refs, heads=heads, size=size,...  43.5 us
    pallas_call x1, Pallas kernels, attend_back(): pl.pallas_call(lambda *refs: back_kernel(*refs, heads=heads, size=size, p...  42.6 us
    reduce_scatter x4, waiting for transfers between devices, scattered(): return lax.psum_scatter(grad, 'fsdp', scatter_dimension=0, tiled=True)  39.9 us
    dot_general x4, matrix products, inner_rows(): lax.dot_general(left, right, (((0,), (0,)), ((), ())), preferred_element_...  34.5 us
    dot_general x4, matrix products, times_trans(): lax.dot_general(left, right, (((1,), (1,)), ((), ())), preferred_element_...  29.1 us
    all_to_all x1, blocking collectives, swap(): return lax.all_to_all(value, 'cp', 0, 0, tiled=True)  22.4 us
  transfers between devices with their start and end apart: 12, of which 8 were waited for; matrix products, arithmetic and copies ran while one was open for 16% of the time, Pallas kernels for 6%

profile of v1, /device:TPU:0, one launch (start us, length us, event | category | flops | bytes accessed | tf_op | source)
XLA Modules:
  0.0 745.6 jit_solution(6662081640879981085)
XLA Ops:
  16.8 8.4 %all-gather.7.cloned.1.call-done = bf16[768,2304]{1,0:T(8,128)(2,1)} async-done(((bf16[384,2304]{1,0:T(8,128)(2,1)}), bf16[768,2304]{1,0:T(8,128)(2,1)}) %all-gather.7.cloned.1.call-update) | async-done | bytes 3538960 | tf_op jit(solution)/shard_map/all_gather | solution.py:292
  25.1 7.4 add_convert_fusion
  32.6 6.7 copy.51
  44.3 9.1 %reshape.288 = bf16[4,2,512,576]{2,1,3,0:T(2,128)(2,1)} reshape(bf16[4,1024,3,192]{1,3,2,0:T(8,128)(2,1)} %copy.52) | data formatting | bytes 9437184 | tf_op jit(solution)/shard_map/reshape | solution.py:311
  64.8 52.7 %all-to-all-done = bf16[4,2,512,576]{2,3,1,0:T(8,128)(2,1)} async-done(((bf16[4,2,512,576]{2,3,1,0:T(8,128)(2,1)}), bf16[4,2,512,576]{2,3,1,0:T(8,128)(2,1)}, u32[]{:S(2)}, u32[]{:S(2)}) %all-to-all-start) | async-done | bytes 4718624 | tf_op jit(solution)/shard_map/all_to_all | solution.py:257
  117.5 7.7 %copy.54.refs_2_ = bf16[4,2,512,576]{3,2,1,0:T(8,128)(2,1)} copy(bf16[4,2,512,576]{2,3,1,0:T(8,128)(2,1)} %all-to-all-done) | data formatting | bytes 9437184 | tf_op jit(solution)/shard_map/all_to_all | solution.py:257
  127.7 43.5 %attend.1 = (bf16[4,2,512,192]{3,2,1,0:T(8,128)(2,1)S(1)}, f32[2,192,2048]{2,1,0:T(8,128)S(1)}, f32[2,3,2048]{2,1,0:T(4,128)S(1)}) custom-call(s32[2,8]{1,0:T(2,128)S(1)} %and_select_fusion.refs_0_, s32[2,1,2048]{2,1,0:T(1,128)S(1)} %broadcast_in_dim.64.refs_1_, bf16[4,2,512,576]{3,2,1,0:T(8,128)(2,1)S(1)} %copy-done), custom_call_target="tpu_custom_call" | custom-call | flops 20000000000 | bytes 12000000 | tf_op jit(solution)/shard_map/attend/pallas_call | solution.py:203
  180.1 17.1 %all-to-all-done.1 = bf16[4,2,512,192]{2,3,1,0:T(8,128)(2,1)} async-done(((bf16[4,2,512,192]{2,3,1,0:T(8,128)(2,1)}), bf16[4,2,512,192]{2,3,1,0:T(8,128)(2,1)}, u32[]{:S(2)}, u32[]{:S(2)}) %all-to-all-start.1) | async-done | bytes 1572896 | tf_op jit(solution)/shard_map/all_to_all | solution.py:257
  205.1 11.1 %fusion.37 = f32[1024,3072]{1,0:T(8,128)} fusion(bf16[768,3072]{1,0:T(8,128)(2,1)} %all-gather.11.cloned.1.call-done, f32[1024,768]{1,0:T(8,128)} %copy-done.11, f32[768]{0:T(1024)S(1)} %reshape.314, f32[768]{0:T(1024)S(1)} %reshape.313, f32[1024]{0:T(1024)S(1)} %fusion.32, f32[1024]{0:T(1024)S(1)} %broadcast_multiply_fusion), kind=kOutput, calls=%fused_computation.103 | convolution fusion | flops 4835770368 | bytes 20461568 | tf_op jit(solution)/shard_map/dot_general | solution.py:318
  216.2 17.5 %fusion.44 = (bf16[3072]{0:T(1024)(128)(2,1)S(1)}, bf16[1024,3072]{1,0:T(8,128)(2,1)S(1)}) fusion(bf16[1024,768]{1,0:T(8,128)(2,1)S(1)} %bitcast.104, bf16[3072,768]{1,0:T(8,128)(2,1)} %all-gather.13.cloned.1.call-done, f32[1024,3072]{1,0:T(8,128)} %fusion.37, f32[3072]{0:T(1024)S(1)} %reshape.315), kind=kOutput, calls=%fused_computation.109 | convolution fusion | flops 4913624064 | bytes 25184256 | tf_op jit(solution)/shard_map/dot_general | solution.py:32
  244.7 22.4 %all_to_all.20 = bf16[4,2,512,192]{2,3,1,0:T(8,128)(2,1)} all-to-all(bf16[4,2,512,192]{2,3,1,0:T(8,128)(2,1)S(1)} %bitcast.106), channel_id=1, replica_groups=mesh['cp'=4,'fsdp'=2,'rep'=4] {'cp'}, dimensions={0} | all-to-all | bytes 3145728 | tf_op jit(solution)/shard_map/all_to_all | solution.py:257
  271.7 42.6 %attend_back.1 = bf16[4,2,512,576]{3,2,1,0:T(8,128)(2,1)} custom-call(s32[2,8]{1,0:T(2,128)S(1)} %and_select_fusion.refs_0_, s32[2,1,2048]{2,1,0:T(1,128)S(1)} %broadcast_in_dim.64.refs_1_, bf16[4,2,512,576]{3,2,1,0:T(8,128)(2,1)} %copy.54.refs_2_, bf16[4,2,512,192]{3,2,1,0:T(8,128)(2,1)S(1)} %copy.59.refs_3_, f32[2,192,2048]{2,1,0:T(8,128)S(1)} %copy-done.2, ...), custom_call_target="tpu_custom_call" | custom-call | flops 49999998976 | bytes 18000000 | tf_op jit(solution)/shard_map/attend_back/pallas_call | solution.py:232
  314.3 7.6 %copy.60 = bf16[4,2,512,576]{2,3,1,0:T(8,128)(2,1)} copy(bf16[4,2,512,576]{3,2,1,0:T(8,128)(2,1)} %attend_back.1) | data formatting | bytes 9437184 | tf_op jit(solution)/shard_map/attend_back/pallas_call | solution.py:232
  331.6 44.7 %all-to-all-done.3 = bf16[4,2,512,576]{2,3,1,0:T(8,128)(2,1)} async-done(((bf16[4,2,512,576]{2,3,1,0:T(8,128)(2,1)}), bf16[4,2,512,576]{2,3,1,0:T(8,128)(2,1)}, u32[]{:S(2)}, u32[]{:S(2)}) %all-to-all-start.3) | async-done | bytes 4718624 | tf_op jit(solution)/shard_map/all_to_all | solution.py:257
  376.3 9.4 %copy.61 = bf16[4,2,512,576]{2,1,3,0:T(2,128)(2,1)} copy(bf16[4,2,512,576]{2,3,1,0:T(8,128)(2,1)} %all-to-all-done.3) | data formatting | bytes 9437184 | tf_op jit(solution)/shard_map/all_to_all | solution.py:257
  385.7 8.9 %reshape.295 = bf16[4,1024,3,192]{1,3,2,0:T(8,128)(2,1)} reshape(bf16[4,2,512,576]{2,1,3,0:T(2,128)(2,1)} %copy.61) | data formatting | bytes 9437184 | tf_op jit(solution)/shard_map/reshape | solution.py:350
  413.5 10.3 %convolution_convert_fusion.1 = bf16[768,3072]{1,0:T(8,128)(2,1)} fusion(bf16[1024,3072]{1,0:T(8,128)(2,1)} %copy-done.47, f32[1024,768]{1,0:T(8,128)} %copy-done.11, f32[768]{0:T(1024)S(1)} %reshape.314, f32[768]{0:T(1024)S(1)} %reshape.313, f32[1024]{0:T(1024)S(1)} %fusion.32, f32[1024]{0:T(1024)S(1)} %broadcast_multiply_fusion), kind=kOutput, calls=%fused_computation.13 | convolution fusion | flops 4838129664 | bytes 14170112 | tf_op jit(solution)/shard_map/dot_general | solution.py:26
  423.9 12.6 %convolution_convert_fusion = bf16[3072,768]{1,0:T(8,128)(2,1)} fusion(bf16[1024,768]{1,0:T(8,128)(2,1)S(1)} %bitcast.105, f32[1024,3072]{1,0:T(8,128)} %fusion.37, f32[3072]{0:T(1024)S(1)} %reshape.315), kind=kOutput, calls=%fused_computation.12 | convolution fusion | flops 4865654784 | bytes 18886656 | tf_op jit(solution)/shard_map/dot_general | solution.py:26
  437.8 7.8 %convolution_convert_fusion.2 = bf16[768,2304]{1,0:T(8,128)(2,1)} fusion(bf16[1024,768]{1,0:T(8,128)(2,1)S(1)} %bitcast.113, bf16[1024,2304]{0,1:T(8,128)(2,1)} %bitcast.109), kind=kOutput, calls=%fused_computation.14 | convolution fusion | flops 3625648128 | bytes 9830400 | tf_op jit(solution)/shard_map/dot_general | solution.py:26
  445.7 8.3 %reduce-scatter.9.cloned.1.call-done = bf16[384,3072]{1,0:T(8,128)(2,1)} async-done(((bf16[768,3072]{1,0:T(8,128)(2,1)}), bf16[384,3072]{1,0:T(8,128)(2,1)}) %reduce-scatter.9.cloned.1.call-update) | async-done | bytes 2359312 | tf_op jit(solution)/shard_map/reduce_scatter | solution.py:342
  454.0 16.1 %reduce-scatter.11.cloned.1.call-done = bf16[1536,768]{1,0:T(8,128)(2,1)} async-done(((bf16[3072,768]{1,0:T(8,128)(2,1)}), bf16[1536,768]{1,0:T(8,128)(2,1)}) %reduce-scatter.11.cloned.1.call-update) | async-done | bytes 2359312 | tf_op jit(solution)/shard_map/reduce_scatter | solution.py:342
  470.1 15.5 %reduce-scatter.7.cloned.1.call-done = bf16[384,2304]{1,0:T(8,128)(2,1)} async-done(((bf16[768,2304]{1,0:T(8,128)(2,1)}), bf16[384,2304]{1,0:T(8,128)(2,1)}) %reduce-scatter.7.cloned.1.call-update) | async-done | bytes 1769488 | tf_op jit(solution)/shard_map/reduce_scatter | solution.py:342
  486.2 13.7 %add_convert_fusion.2 = bf16[1024,768]{1,0:T(8,128)(2,1)} fusion(f32[1024,768]{1,0:T(8,128)} %copy-done.11, bf16[3072,768]{1,0:T(8,128)(2,1)} %all-gather.13.cloned.1.call-done, f32[768]{0:T(1024)S(1)} %reshape.316, f32[1024,3072]{1,0:T(8,128)} %fusion.37, f32[3072]{0:T(1024)S(1)} %reshape.315), kind=kOutput, calls=%fused_computation.40 | convolution fusion | flops 4865654784 | bytes 22035456 | tf_op jit(solution)/shard_map/dot_general | solution.py:320
  502.6 222.2 %all-reduce.4.cloned.1.call-done = (bf16[400,768]{1,0:T(8,128)(2,1)}, bf16[384,2304]{1,0:T(8,128)(2,1)}, bf16[384,3072]{1,0:T(8,128)(2,1)}, bf16[1536,768]{1,0:T(8,128)(2,1)}) async-done(((bf16[400,768]{1,0:T(8,128)(2,1)}, bf16[384,2304]{1,0:T(8,128)(2,1)}, bf16[384,3072]{1,0:T(8,128)(2,1)}, bf16[1536,768]{1,0:T(8,128)(2,1)}), (bf16[400,768]{1,0:T(8,128)(2,1)}, bf16[384,2304]{1,0:T(8,128)(2,1)}, ...) | async-done | bytes 7102480 | tf_op jit(solution)/shard_map/psum | solution.py:370
  (217 shorter events, 107.7 us)
Async XLA Ops:
  7.3 6.7 copy-start.3
  7.3 17.9 %all-gather.7.cloned.1.call-start = ((), (), s32[]{:S(2)}) async-start(), calls=%async_computation.8 | async-start | bytes 5308416 | tf_op jit(solution)/shard_map/all_gather | solution.py:292
  8.0 191.9 %all-gather.9.cloned.1.call-start = ((), (), s32[]{:S(2)}) async-start(), calls=%async_computation.9 | async-start | bytes 1769472 | tf_op jit(solution)/shard_map/all_gather | solution.py:293
  8.8 196.3 %all-gather.11.cloned.1.call-start = ((), (), s32[]{:S(2)}) async-start(), calls=%async_computation.10 | async-start | bytes 7077888 | tf_op jit(solution)/shard_map/all_gather | solution.py:294
  16.1 16.5 %copy-start.22 = (f32[1024]{0:T(1024)}, f32[1024]{0:T(1024)S(1)}, u32[]{:S(2)}) copy-start(f32[1024]{0:T(1024)S(1)} %rsqrt.25) | copy-start | bytes 12292
  16.1 16.5 %copy-start.24 = (f32[1,4,2,128]{3,1,2,0:T(4,128)}, f32[1,4,2,128]{3,1,2,0:T(4,128)S(1)}, u32[]{:S(2)}) copy-start(f32[1,4,2,128]{3,1,2,0:T(4,128)S(1)} %copy.66) | copy-start | bytes 12292
  58.7 58.8 %all-to-all-start = ((bf16[4,2,512,576]{2,3,1,0:T(8,128)(2,1)}), bf16[4,2,512,576]{2,3,1,0:T(8,128)(2,1)}, u32[]{:S(2)}, u32[]{:S(2)}) async-start(bf16[4,2,512,576]{2,3,1,0:T(8,128)(2,1)} %copy.53), calls=%async_computation | async-start | bytes 9437184 | tf_op jit(solution)/shard_map/all_to_all | solution.py:257
  63.8 152.4 %all-gather.13.cloned.1.call-start = ((), (), s32[]{:S(2)}) async-start(), calls=%async_computation.11 | async-start | bytes 7077888 | tf_op jit(solution)/shard_map/all_gather | solution.py:295
  175.0 24.9 %copy-start.4 = (bf16[2,512,768]{2,1,0:T(8,128)(2,1)S(1)}, bf16[2,512,768]{2,1,0:T(8,128)(2,1)}, u32[]{:S(2)}) copy-start(bf16[2,512,768]{2,1,0:T(8,128)(2,1)} %param.16) | copy-start | bytes 4718596
  175.0 22.2 %all-to-all-start.1 = ((bf16[4,2,512,192]{2,3,1,0:T(8,128)(2,1)}), bf16[4,2,512,192]{2,3,1,0:T(8,128)(2,1)}, u32[]{:S(2)}, u32[]{:S(2)}) async-start(bf16[4,2,512,192]{2,3,1,0:T(8,128)(2,1)} %copy.55), calls=%async_computation.1 | async-start | bytes 3145728 | tf_op jit(solution)/shard_map/all_to_all | solution.py:257
  205.1 11.1 %copy-start.9 = (bf16[2,512,768]{2,1,0:T(8,128)(2,1)S(1)}, bf16[2,512,768]{2,1,0:T(8,128)(2,1)}, u32[]{:S(2)}) copy-start(bf16[2,512,768]{2,1,0:T(8,128)(2,1)} %param.31) | copy-start | bytes 4718596
  216.2 17.5 %copy-start.12 = (f32[1024,768]{1,0:T(8,128)S(1)}, f32[1024,768]{1,0:T(8,128)}, u32[]{:S(2)}) copy-start(f32[1024,768]{1,0:T(8,128)} %copy-done.11) | copy-start | bytes 9437188
  216.2 17.5 %copy-start.44 = (bf16[768,3072]{1,0:T(8,128)(2,1)S(1)}, bf16[768,3072]{1,0:T(8,128)(2,1)}, u32[]{:S(2)}) copy-start(bf16[768,3072]{1,0:T(8,128)(2,1)} %all-gather.11.cloned.1.call-done) | copy-start | bytes 14155780
  321.9 5.9 copy-start.18
  321.9 54.4 %all-to-all-start.3 = ((bf16[4,2,512,576]{2,3,1,0:T(8,128)(2,1)}), bf16[4,2,512,576]{2,3,1,0:T(8,128)(2,1)}, u32[]{:S(2)}, u32[]{:S(2)}) async-start(bf16[4,2,512,576]{2,3,1,0:T(8,128)(2,1)} %copy.60), calls=%async_computation.3 | async-start | bytes 9437184 | tf_op jit(solution)/shard_map/all_to_all | solution.py:257
  327.1 118.6 %reduce-scatter.5.cloned.1.call-start = ((), (), s32[]{:S(2)}) async-start(), calls=%async_computation.12 | async-start | bytes 1843200 | tf_op jit(solution)/shard_map/reduce_scatter | solution.py:342
  398.9 8.3 %copy-start.15 = (bf16[1024,3,4,192]{0,3,2,1:T(8,128)(2,1)}, bf16[1024,3,4,192]{0,3,2,1:T(8,128)(2,1)S(1)}, u32[]{:S(2)}) copy-start(bf16[1024,3,4,192]{0,3,2,1:T(8,128)(2,1)S(1)} %copy.62) | copy-start | bytes 14155780
  402.6 6.3 copy-start.23
  413.4 40.5 %reduce-scatter.9.cloned.1.call-start = ((), (), s32[]{:S(2)}) async-start(), calls=%async_computation.14 | async-start | bytes 7077888 | tf_op jit(solution)/shard_map/reduce_scatter | solution.py:342
  423.9 46.2 %reduce-scatter.11.cloned.1.call-start = ((), (), s32[]{:S(2)}) async-start(), calls=%async_computation.15 | async-start | bytes 7077888 | tf_op jit(solution)/shard_map/reduce_scatter | solution.py:342
  436.5 49.0 %reduce-scatter.7.cloned.1.call-start = ((), (), s32[]{:S(2)}) async-start(), calls=%async_computation.13 | async-start | bytes 5308416 | tf_op jit(solution)/shard_map/reduce_scatter | solution.py:342
  445.6 279.1 %all-reduce.4.cloned.1.call-start = ((), (), s32[]{:S(2)}) async-start(), calls=%async_computation.16 | async-start | bytes 14204928 | tf_op jit(solution)/shard_map/psum | solution.py:370
  486.2 13.7 %copy-start.8 = (f32[1024,768]{1,0:T(8,128)S(1)}, f32[1024,768]{1,0:T(8,128)}, u32[]{:S(2)}) copy-start(f32[1024,768]{1,0:T(8,128)} %copy-done.7) | copy-start | bytes 9437188
  486.2 13.7 %copy-start.14 = (f32[1024,768]{1,0:T(8,128)S(1)}, f32[1024,768]{1,0:T(8,128)}, u32[]{:S(2)}) copy-start(f32[1024,768]{1,0:T(8,128)} %copy-done.13) | copy-start | bytes 9437188
  (36 other events, 97.5 us)
Sparse Core Ops, SparseCore 0:
  9.7 15.4 all-gather.6
  26.7 10.3 all-gather.8
  38.7 15.5 all-gather.10
  65.9 16.1 all-gather.12
  413.6 23.7 reduce-scatter.4
  440.1 13.7 reduce-scatter.8
  456.3 13.7 reduce-scatter.10
  473.0 12.5 reduce-scatter.6
  492.0 232.7 all-reduce.3
